TPU v7x, 32 devices: a whole 2x2x4 slice. The times are simulated.
32 devices in a mesh: tm: 4 (over y, core), chan: 8 (over z, x).
Axes of the slice: x: 2, y: 2, z: 4, core: 2. Of those that a mesh axis runs over, the one named last changes fastest.
Arguments:
- recordings: float32 [4, 256, 8, 512], P('tm', None, 'chan')
- gap_start: int32 [4, 256, 8], P('tm', None, 'chan'), may hold values from 0 to 511
- dropout_extent: int32 [4, 256, 8], P('tm', None, 'chan'), may hold values from 0 to 256
- filter_taps: float32 [128], replicated, may hold values from -0.5 to 0.5
- source_channel: int32 [32], P('chan'), may hold values from 0 to 255
- receiver_block: int32 [32], P('chan'), may hold values from 0 to 3
Outputs:
- stacks: float32 [128, 32, 1024], P('tm', 'chan')
All inputs are finite; a program needn't handle non-finite values.
Results may differ from a plain program's by a relative error of at most 0.0031.
Values may be sent and summed in bfloat16 or wider, within the bound.
No kernel may reach another device: no remote copies, remote signals or barrier semaphores. Data moves between devices by JAX's collectives and lax.ppermute only.
A program may use at most 64 MiB of HBM per device.

v0:
```python
import math
import jax
import jax.numpy as jnp
import numpy as np
from jax import lax
from jax.sharding import PartitionSpec as P

BLOCK = 128
MAX_LAG = 512


def passed_along(block, axis, distance):
    devices = range(lax.axis_size(axis))
    route = [(i - distance, i) for i in devices if i - distance in devices]
    return lax.ppermute(block, axis, route)


def valid_mask(starts, lengths, sample_count):
    position = jnp.arange(sample_count, dtype=jnp.int32)
    inside = (position >= starts[..., None]) & (position < starts[..., None] + lengths[..., None])
    return jnp.where(inside, 0.0, 1.0).astype(jnp.float32)


def fir_filter(signal, filter_taps):
    tap_count = filter_taps.shape[0]
    channel_count, sample_count = signal.shape
    pieces = signal.reshape(channel_count, sample_count // tap_count, tap_count)
    earlier = jnp.concatenate([jnp.zeros_like(pieces[:, :1]), pieces[:, :-1]], axis=1)
    position = jnp.arange(tap_count, dtype=jnp.int32)
    offset = position[None, :] - position[:, None]
    present_filter_tap = jnp.where(
        offset >= 0, filter_taps[jnp.clip(offset, 0, tap_count - 1)], 0.0
    )
    carried_tap = jnp.where(
        offset < 0, filter_taps[jnp.clip(offset + tap_count, 0, tap_count - 1)], 0.0
    )
    result = jnp.einsum("cki,im->ckm", pieces, present_filter_tap, precision=lax.Precision.HIGHEST)
    result = result + jnp.einsum(
        "cki,im->ckm", earlier, carried_tap, precision=lax.Precision.HIGHEST
    )
    return result.reshape(channel_count, sample_count)


def normalize_traces(filtered, retained_mask):
    counted = jnp.sum(retained_mask, axis=-1, keepdims=True)
    mean_square = jnp.sum(filtered * filtered * retained_mask, axis=-1, keepdims=True) / counted
    return (filtered * retained_mask * lax.rsqrt(mean_square + 1e-05)).astype(jnp.bfloat16)


def correlate_batch(sources, receivers, max_lag):
    sample_count = sources.shape[-1]
    tile_width = math.gcd(math.gcd(max_lag, sample_count), 128)
    tile_count = sample_count // tile_width + 1
    edge = jnp.zeros((sources.shape[0], tile_width), sources.dtype)
    source_padded = jnp.concatenate([edge, sources, edge], axis=1)
    row_table = (
        np.arange(tile_count * tile_width)[:, None] - np.arange(tile_width)[None, :] + tile_width
    )
    lag_tiles = source_padded[:, row_table]
    lag_pad = jnp.zeros((receivers.shape[0], receivers.shape[1], max_lag), receivers.dtype)
    receivers_padded = jnp.concatenate([lag_pad, receivers, lag_pad], axis=2)
    columns = []
    for lag_block in range(2 * max_lag // tile_width):
        segment_taper = receivers_padded[
            :, :, lag_block * tile_width : lag_block * tile_width + tile_count * tile_width
        ]
        columns.append(
            jnp.einsum("scz,szu->csu", segment_taper, lag_tiles, preferred_element_type=jnp.float32)
        )
    return jnp.concatenate(columns, axis=2)


def select_blocks(blocks, receiver_block, pair_count):
    picked = [
        lax.dynamic_slice_in_dim(blocks, receiver_block[pair_index], 1, axis=0)
        for pair_index in range(pair_count)
    ]
    return jnp.concatenate(picked, axis=0)


def neighbour_blocks(owned_rows):
    return passed_along(owned_rows, "chan", -1)


def local(recordings, gap_start, dropout_extent, filter_taps, source_channel, receiver_block):
    traces = recordings[0, :, 0, :]
    retained_mask = valid_mask(gap_start[0, :, 0], dropout_extent[0, :, 0], traces.shape[1])
    filtered = fir_filter(traces * retained_mask, filter_taps)
    normalized = normalize_traces(filtered, retained_mask)
    round_count, sample_count = normalized.shape
    regrouped = lax.all_to_all(
        normalized.reshape(round_count, 1, sample_count),
        "chan",
        split_axis=0,
        concat_axis=1,
        tiled=True,
    )
    owned_rows = regrouped.reshape(round_count, sample_count)
    sources = owned_rows[source_channel]
    segment_count = lax.axis_size("tm")
    factor = 1.0 / math.sqrt(sample_count * segment_count)
    pair_count = sources.shape[0]
    block_count = round_count // BLOCK
    following = neighbour_blocks(owned_rows)
    blocks = jnp.concatenate([owned_rows, following], axis=0).reshape(
        2 * block_count, BLOCK, sample_count
    )
    receivers = select_blocks(blocks, receiver_block, pair_count)
    stack_terms = correlate_batch(sources, receivers, MAX_LAG) * factor
    stacks = lax.psum_scatter(stack_terms, "tm", scatter_dimension=0, tiled=True)
    return stacks


def solution(mesh):
    return jax.shard_map(
        local,
        mesh=mesh,
        in_specs=(
            P("tm", None, "chan", None),
            P("tm", None, "chan"),
            P("tm", None, "chan"),
            P(),
            P("chan"),
            P("chan"),
        ),
        out_specs=P("tm", "chan", None),
        check_vma=False,
    )
```

profile of v0, /device:TPU:0, one launch (start us, length us, event | category | flops | bytes accessed | tf_op | source)
XLA Modules:
  0.0 605.1 jit_solution(15314912430270999718)
XLA Ops:
  6.5 0.0 copy-start
  6.6 1.2 copy.46
  7.9 0.0 copy-done
  7.9 97.2 %gather_fusion = f32[16384]{0:T(1024)S(1)} fusion(f32[128]{0:T(128)S(1)} %copy-done, s32[16384]{0:T(1024)S(1)} %fusion.21), kind=kCustom, calls=%fused_computation | custom fusion | bytes 196608 | tf_op jit(solution)/shard_map/gather | solution.py:32
  105.1 0.0 copy-start.2
  105.1 0.0 copy-start.4
  105.1 97.2 %gather_fusion.1 = f32[16384]{0:T(1024)S(1)} fusion(f32[128]{0:T(128)S(1)} %copy-done, s32[16384]{0:T(1024)S(1)} %fusion.23), kind=kCustom, calls=%fused_computation.1 | custom fusion | bytes 196608 | tf_op jit(solution)/shard_map/gather | solution.py:35
  202.3 0.0 copy-done.2
  202.3 0.0 copy-done.4
  202.4 0.2 select_reduce_fusion
  202.6 0.2 select_multiply_fusion.1
  202.8 0.6 fusion.25
  203.4 0.0 copy-start.1
  203.4 0.7 fusion.16
  204.2 0.2 copy.63
  204.4 0.2 multiply_convert_fusion
  204.6 0.5 broadcast.235
  205.1 0.8 reduce.1
  205.9 0.9 reshape.270
  206.8 7.2 %all-to-all-start = ((bf16[8,2,8192]{2,1,0:T(2,128)(2,1)}), bf16[8,2,8192]{2,1,0:T(2,128)(2,1)S(1)}, u32[]{:S(2)}, u32[]{:S(2)}) async-start(bf16[8,2,8192]{2,1,0:T(2,128)(2,1)} %reshape.270), calls=%async_computation | async-start | bytes 524288 | tf_op jit(solution)/shard_map/all_to_all | solution.py:91
  214.0 0.0 all-reduce.6.cloned.1.call-start
  214.2 8.8 %all-to-all-done = bf16[8,2,8192]{2,1,0:T(2,128)(2,1)S(1)} async-done(((bf16[8,2,8192]{2,1,0:T(2,128)(2,1)}), bf16[8,2,8192]{2,1,0:T(2,128)(2,1)S(1)}, u32[]{:S(2)}, u32[]{:S(2)}) %all-to-all-start) | async-done | bytes 262176 | tf_op jit(solution)/shard_map/all_to_all | solution.py:91
  223.0 0.3 reshape.271
  223.3 0.2 copy.66
  223.4 1.3 collective-permute-start
  224.7 0.0 copy-done.3
  224.8 0.7 fusion.47
  233.0 0.6 gather_fusion.2
  233.6 0.2 copy.54
  233.8 286.2 %gather_fusion.3 = bf16[81920,4]{1,0:T(8,128)(2,1)} fusion(bf16[4,768]{0,1:T(8,128)(2,1)S(1)} %copy.54, s32[81920]{0:T(1024)S(1)} %broadcast_clamp_fusion), kind=kCustom, calls=%fused_computation.3 | custom fusion | bytes 1638400 | tf_op jit(solution)/shard_map/gather | solution.py:59
  520.0 19.5 %copy.55 = bf16[640,128,4]{0,1,2:T(8,128)(2,1)S(1)} copy(bf16[640,128,4]{2,1,0:T(8,128)(2,1)} %bitcast.95) | data formatting | bytes 1310720 | tf_op jit(solution)/shard_map/gather | solution.py:59
  539.5 0.0 collective-permute-done
  539.6 0.1 pad_maximum_fusion.1
  539.6 0.3 fusion.7
  540.0 0.3 fusion.6
  540.3 0.3 fusion.5
  540.6 0.4 fusion.4
  541.0 0.4 fusion.3
  541.4 0.3 fusion.2
  541.7 0.3 fusion.1
  542.1 0.3 fusion
  542.4 0.2 broadcast_multiply_fusion
  542.6 2.0 copy.56
  544.6 0.0 all-reduce.6.cloned.1.call-update
  544.7 0.6 copy-done.6
  545.3 0.6 dynamic-slice
  546.5 49.9 %all-reduce.6.cloned.1.call-done = f32[128,4,1024]{2,1,0:T(4,128)} async-done(((f32[128,4,1024]{2,1,0:T(4,128)}), f32[128,4,1024]{2,1,0:T(4,128)}) %all-reduce.6.cloned.1.call-update) | async-done | bytes 2097168
  596.4 1.9 constant_dynamic-slice_fusion.4
  (18 shorter events, 0.3 us)
Async XLA Ops:
  6.5 1.3 copy-start
  105.1 97.2 %copy-start.2 = (s32[1,256,1]{1,2,0:T(1,128)S(1)}, s32[1,256,1]{1,2,0:T(1,128)}, u32[]{:S(2)}) copy-start(s32[1,256,1]{1,2,0:T(1,128)} %param.9) | copy-start | bytes 3076
  105.1 97.2 %copy-start.4 = (s32[1,256,1]{1,2,0:T(1,128)S(1)}, s32[1,256,1]{1,2,0:T(1,128)}, u32[]{:S(2)}) copy-start(s32[1,256,1]{1,2,0:T(1,128)} %param.10) | copy-start | bytes 3076
  203.4 10.7 %copy-start.1 = (s32[81920]{0:T(1024)S(1)}, s32[81920]{0:T(1024)}, u32[]{:S(2)}) copy-start(s32[81920]{0:T(1024)} %constant.48) | copy-start | bytes 983044
  204.2 10.0 %copy-start.5 = (s32[4]{0:T(128)S(1)}, s32[4]{0:T(128)}, u32[]{:S(2)}) copy-start(s32[4]{0:T(128)} %param.12) | copy-start | bytes 52
  205.1 19.6 %copy-start.3 = (s32[4]{0:T(128)S(1)}, s32[4]{0:T(128)}, u32[]{:S(2)}) copy-start(s32[4]{0:T(128)} %param.13) | copy-start | bytes 52
  206.8 16.2 %all-to-all-start = ((bf16[8,2,8192]{2,1,0:T(2,128)(2,1)}), bf16[8,2,8192]{2,1,0:T(2,128)(2,1)S(1)}, u32[]{:S(2)}, u32[]{:S(2)}) async-start(bf16[8,2,8192]{2,1,0:T(2,128)(2,1)} %reshape.270), calls=%async_computation | async-start | bytes 524288 | tf_op jit(solution)/shard_map/all_to_all | solution.py:91
  214.0 382.4 %all-reduce.6.cloned.1.call-start = ((), (), s32[]{:S(2)}) async-start(), calls=%async_computation.1 | async-start | bytes 4194304
  223.4 316.0 %collective-permute-start = (bf16[256,512]{1,0:T(8,128)(2,1)S(1)}, bf16[256,512]{1,0:T(8,128)(2,1)S(1)}, u32[]{:S(2)}, u32[]{:S(2)}) collective-permute-start(bf16[256,512]{1,0:T(8,128)(2,1)S(1)} %bitcast.99), channel_id=1, source_target_pairs={{1,0},{2,1},{3,2},{4,3},{5,4},{6,5},{7,6},{9,8},{10,9},{11,10},{12... | collective-permute-start | bytes 786440 | tf_op jit(solution)/shard_map/ppermute | solution.py:15
  544.6 0.7 copy-start.6
Sparse Core Ops, SparseCore 0:
  544.8 51.5 all-reduce.5
where the time goes:
time: 606 us; the launch traced here: 605 us
  local copies, waits for them, and re-layouts  510 us (84%)
  waiting for transfers between devices  58.7 us (10%)
  between operations  21.9 us (4%)
  starting transfers between devices  8.58 us (1%)
    gather x2, local copies, waits for them, and re-layouts, correlate_batch(): lag_tiles = source_padded[:, row_table]  306 us
    gather x1, local copies, waits for them, and re-layouts, fir_filter(): filter_taps[jnp.clip(offset, 0, tap_count - 1)]  97.2 us
    gather x1, local copies, waits for them, and re-layouts, fir_filter(): filter_taps[jnp.clip(offset + tap_count, 0, tap_count - 1)]  97.2 us
    unnamed x2, waiting for transfers between devices  49.9 us
  transfers between devices with their start and end apart: 3, of which 2 were waited for; matrix products, arithmetic and copies ran while one was open for 51% of the time, Pallas kernels for 0%

commit v1 on v0

--- a/solution.py
+++ b/solution.py
@@ -88,13 +88,10 @@
     filtered = fir_filter(traces * retained_mask, filter_taps)
     normalized = normalize_traces(filtered, retained_mask)
     round_count, sample_count = normalized.shape
-    regrouped = lax.all_to_all(
-        normalized.reshape(round_count, 1, sample_count),
-        "chan",
-        split_axis=0,
-        concat_axis=1,
-        tiled=True,
-    )
+    xx = normalized.reshape(round_count, 1, sample_count)
+    everything = jnp.split(xx, lax.axis_size("chan"), axis=0)
+    item_now = lax.all_to_all(jnp.stack(everything), concat_axis=0, split_axis=0, axis_name="chan")
+    regrouped = jnp.concatenate(item_now, axis=1)
     owned_rows = regrouped.reshape(round_count, sample_count)
     sources = owned_rows[source_channel]
     segment_count = lax.axis_size("tm")

time: 606 us -> 606 us (level)
  transfers between devices with their start and end apart: 3 -> 3, of which waited for: 2 -> 2; matrix products, arithmetic and copies ran while one was open for 51% -> 50% of each run, Pallas kernels for 0% -> 0%
where the time goes in v1:
time: 606 us; the launch traced here: 605 us
  local copies, waits for them, and re-layouts  511 us (84%)
  waiting for transfers between devices  58.7 us (10%)
  between operations  21.9 us (4%)
  starting transfers between devices  8.58 us (1%)
    gather x2, local copies, waits for them, and re-layouts, correlate_batch(): lag_tiles = source_padded[:, row_table]  304 us
    gather x1, local copies, waits for them, and re-layouts, fir_filter(): filter_taps[jnp.clip(offset, 0, tap_count - 1)]  97.2 us
    gather x1, local copies, waits for them, and re-layouts, fir_filter(): filter_taps[jnp.clip(offset + tap_count, 0, tap_count - 1)]  97.2 us
    unnamed x2, waiting for transfers between devices  49.9 us
  transfers between devices with their start and end apart: 3, of which 2 were waited for; matrix products, arithmetic and copies ran while one was open for 50% of the time, Pallas kernels for 0%

profile of v1, /device:TPU:0, one launch (start us, length us, event | category | flops | bytes accessed | tf_op | source)
XLA Modules:
  0.0 605.5 jit_solution(2864777512462318946)
XLA Ops:
  6.6 1.2 copy.25
  7.9 97.2 %gather_fusion = f32[16384]{0:T(1024)S(1)} fusion(f32[128]{0:T(128)S(1)} %copy-done, s32[16384]{0:T(1024)S(1)} %fusion.22), kind=kCustom, calls=%fused_computation | custom fusion | bytes 196608 | tf_op jit(solution)/shard_map/gather | solution.py:32
  105.1 0.0 copy-start.2
  105.1 0.0 copy-start.4
  105.1 97.2 %gather_fusion.1 = f32[16384]{0:T(1024)S(1)} fusion(f32[128]{0:T(128)S(1)} %copy-done, s32[16384]{0:T(1024)S(1)} %fusion.24), kind=kCustom, calls=%fused_computation.1 | custom fusion | bytes 196608 | tf_op jit(solution)/shard_map/gather | solution.py:35
  202.4 0.2 select_reduce_fusion
  202.6 0.2 select_multiply_fusion.2
  202.8 0.6 fusion.26
  203.4 0.0 copy-start.1
  203.4 0.7 fusion.16
  204.2 0.0 copy-start.3
  204.2 0.2 copy.30
  204.4 0.2 fusion.18
  204.6 0.6 fusion.39
  205.2 0.6 fusion.38
  205.8 0.6 fusion.37
  206.4 0.6 fusion.36
  207.1 0.6 fusion.35
  207.7 0.6 fusion.34
  208.3 0.6 fusion.33
  208.9 0.6 fusion.32
  209.5 7.2 %all-to-all-start = ((bf16[8,32,1,512]{3,1,2,0:T(8,128)(2,1)}), bf16[8,32,1,512]{3,1,2,0:T(8,128)(2,1)S(1)}, u32[]{:S(2)}, u32[]{:S(2)}) async-start(bf16[8,32,1,512]{3,1,2,0:T(8,128)(2,1)} %fusion.32), calls=%async_computation | async-start | bytes 524288 | tf_op jit(solution)/shard_map/all_to_all | solution.py:93
  216.8 0.0 all-reduce.6.cloned.1.call-start
  216.9 8.8 %all-to-all-done = bf16[8,32,1,512]{3,1,2,0:T(8,128)(2,1)S(1)} async-done(((bf16[8,32,1,512]{3,1,2,0:T(8,128)(2,1)}), bf16[8,32,1,512]{3,1,2,0:T(8,128)(2,1)S(1)}, u32[]{:S(2)}, u32[]{:S(2)}) %all-to-all-start) | async-done | bytes 262176 | tf_op jit(solution)/shard_map/all_to_all | solution.py:93
  225.7 0.1 copy.42
  225.9 1.3 collective-permute-start
  227.2 0.7 fusion.56
  235.4 0.6 gather_fusion.2
  236.0 0.2 copy.32
  236.2 284.2 %gather_fusion.3 = bf16[81920,4]{1,0:T(8,128)(2,1)} fusion(bf16[4,768]{0,1:T(8,128)(2,1)S(1)} %copy.32, s32[81920]{0:T(1024)S(1)} %broadcast_clamp_fusion), kind=kCustom, calls=%fused_computation.3 | custom fusion | bytes 1638400 | tf_op jit(solution)/shard_map/gather | solution.py:59
  520.3 19.5 %copy.33 = bf16[640,128,4]{0,1,2:T(8,128)(2,1)S(1)} copy(bf16[640,128,4]{2,1,0:T(8,128)(2,1)} %bitcast.125) | data formatting | bytes 1310720 | tf_op jit(solution)/shard_map/gather | solution.py:59
  539.8 0.0 collective-permute-done
  539.9 0.1 pad_maximum_fusion.1
  540.0 0.3 fusion.7
  540.3 0.3 fusion.6
  540.7 0.3 fusion.5
  541.0 0.4 fusion.4
  541.4 0.4 fusion.3
  541.7 0.3 fusion.2
  542.1 0.3 fusion.1
  542.4 0.3 fusion
  542.8 0.2 broadcast_multiply_fusion
  543.0 2.0 copy.34
  545.0 0.0 all-reduce.6.cloned.1.call-update
  545.0 0.6 copy-done.6
  545.6 0.6 dynamic-slice
  546.9 49.9 %all-reduce.6.cloned.1.call-done = f32[128,4,1024]{2,1,0:T(4,128)} async-done(((f32[128,4,1024]{2,1,0:T(4,128)}), f32[128,4,1024]{2,1,0:T(4,128)}) %all-reduce.6.cloned.1.call-update) | async-done | bytes 2097168
  596.8 1.9 constant_dynamic-slice_fusion.4
  (21 shorter events, 0.2 us)
Async XLA Ops:
  6.5 1.3 copy-start
  105.1 97.2 %copy-start.2 = (s32[1,256,1]{1,2,0:T(1,128)S(1)}, s32[1,256,1]{1,2,0:T(1,128)}, u32[]{:S(2)}) copy-start(s32[1,256,1]{1,2,0:T(1,128)} %param.9) | copy-start | bytes 3076
  105.1 97.2 %copy-start.4 = (s32[1,256,1]{1,2,0:T(1,128)S(1)}, s32[1,256,1]{1,2,0:T(1,128)}, u32[]{:S(2)}) copy-start(s32[1,256,1]{1,2,0:T(1,128)} %param.10) | copy-start | bytes 3076
  203.4 13.4 %copy-start.1 = (s32[81920]{0:T(1024)S(1)}, s32[81920]{0:T(1024)}, u32[]{:S(2)}) copy-start(s32[81920]{0:T(1024)} %constant.48) | copy-start | bytes 983044
  204.2 12.7 %copy-start.5 = (s32[4]{0:T(128)S(1)}, s32[4]{0:T(128)}, u32[]{:S(2)}) copy-start(s32[4]{0:T(128)} %param.12) | copy-start | bytes 52
  204.2 23.0 %copy-start.3 = (s32[4]{0:T(128)S(1)}, s32[4]{0:T(128)}, u32[]{:S(2)}) copy-start(s32[4]{0:T(128)} %param.13) | copy-start | bytes 52
  209.5 16.2 %all-to-all-start = ((bf16[8,32,1,512]{3,1,2,0:T(8,128)(2,1)}), bf16[8,32,1,512]{3,1,2,0:T(8,128)(2,1)S(1)}, u32[]{:S(2)}, u32[]{:S(2)}) async-start(bf16[8,32,1,512]{3,1,2,0:T(8,128)(2,1)} %fusion.32), calls=%async_computation | async-start | bytes 524288 | tf_op jit(solution)/shard_map/all_to_all | solution.py:93
  216.8 380.0 %all-reduce.6.cloned.1.call-start = ((), (), s32[]{:S(2)}) async-start(), calls=%async_computation.1 | async-start | bytes 4194304
  225.9 314.0 %collective-permute-start = (bf16[256,512]{1,0:T(8,128)(2,1)S(1)}, bf16[256,512]{1,0:T(8,128)(2,1)S(1)}, u32[]{:S(2)}, u32[]{:S(2)}) collective-permute-start(bf16[256,512]{1,0:T(8,128)(2,1)S(1)} %bitcast.129), channel_id=1, source_target_pairs={{1,0},{2,1},{3,2},{4,3},{5,4},{6,5},{7,6},{9,8},{10,9},{11,10},{12... | collective-permute-start | bytes 786440 | tf_op jit(solution)/shard_map/ppermute | solution.py:15
  545.0 0.7 copy-start.6
Sparse Core Ops, SparseCore 0:
  545.1 51.5 all-reduce.5
